TPU v7x, 32 devices: a whole 2x2x4 slice. The times are simulated.
32 devices in a mesh: wl: 4 (over x, core), gx: 2 (over y), gy: 4 (over z).
Axes of the slice: x: 2, y: 2, z: 4, core: 2. Of those that a mesh axis runs over, the one named last changes fastest.
Arguments:
- forward_efield: float32 [4, 3, 64, 32, 128], P('wl', None, 'gx', 'gy'), may hold values from -6 to 6
- forward_hfield: float32 [4, 3, 64, 32, 128], P('wl', None, 'gx', 'gy'), may hold values from -6 to 6
- adjoint_efield: float32 [4, 3, 64, 32, 128], P('wl', None, 'gx', 'gy'), may hold values from -6 to 6
- adjoint_hfield: float32 [4, 3, 64, 32, 128], P('wl', None, 'gx', 'gy'), may hold values from -6 to 6
- background: float32 [64, 32, 128], P('gx', 'gy'), may hold values from 1 to 4
- design: float32 [8, 64, 32], P('wl', 'gx', 'gy'), may hold values from 1.5 to 6
- source_profile: float32 [4, 64, 32], P('wl', 'gx', 'gy'), may hold values from -24 to 24
- source_layer: int32 [4], P('wl'), may hold values from 4 to 59
- monitor_layer: int32 [4], P('wl'), may hold values from 76 to 123
Outputs:
- final_forward: float32 [4, 3, 64, 32, 128], P('wl', None, 'gx', 'gy')
- final_adjoint: float32 [4, 3, 64, 32, 128], P('wl', None, 'gx', 'gy')
- gradient: float32 [8, 64, 32], P('wl', 'gx', 'gy')
Inputs may be any that keep to these rules, and one draw needn't show every extreme that they name: `source_layer`: a z layer below the design slab. `monitor_layer`: a z layer above the design slab.
All inputs are finite; a program needn't handle non-finite values.
Results may differ from a plain program's by a relative error of at most 0.0001.
Values sent between devices are 32-bit elements; how exact they have to be, the bound alone decides.
No kernel may reach another device: no remote copies, remote signals or barrier semaphores. Data moves between devices by JAX's collectives and lax.ppermute only.
A program may use at most 64 MiB of HBM per device.

v0:
```python
import math
import jax
import jax.numpy as jnp
from jax import lax
from jax.sharding import PartitionSpec as P

Z0 = 64
STEPS = 3
time_step = 0.5


def shifted_2(block, axis, distance):
    devices = range(lax.axis_size(axis))
    route = [(i - distance, i) for i in devices if i - distance in devices]
    return lax.ppermute(block, axis, route)


def neighbours(stacked, upward):
    offset = -1 if upward else 1
    plane_x = stacked[:, :1] if upward else stacked[:, -1:]
    plane_y = stacked[:, :, :1] if upward else stacked[:, :, -1:]
    got_x = shifted_2(plane_x, "gx", offset)
    got_y = shifted_2(plane_y, "gy", offset)
    return (got_x, got_y)


def along(stacked, axis, edge, upward):
    count = stacked.shape[axis]
    if upward:
        shifted = jnp.concatenate([lax.slice_in_dim(stacked, 1, count, axis=axis), edge], axis=axis)
        return shifted - stacked
    shifted = jnp.concatenate([edge, lax.slice_in_dim(stacked, 0, count - 1, axis=axis)], axis=axis)
    return stacked - shifted


def curl(stacked, upward):
    comps, width, height, depth = stacked.shape
    edge_x, edge_y = neighbours(stacked, upward)
    edge_z = jnp.zeros((comps, width, height, 1), jnp.float32)
    along_x = along(stacked, 1, edge_x, upward)
    along_y = along(stacked, 2, edge_y, upward)
    along_z = along(stacked, 3, edge_z, upward)
    return jnp.stack([along_y[2] - along_z[1], along_z[0] - along_x[2], along_x[1] - along_y[0]])


def run_window(efield, hfield, adj_e, adj_h, coef, source_term, omega, monitor_mask, slab_depth):
    slabs = []
    monitors = []
    monitor_pick = monitor_mask[None, None, None, :]
    for turn in range(STEPS):
        hfield = hfield - time_step * curl(efield, True)
        efield = efield + coef * curl(hfield, False)
        signal = jnp.sin(omega * ((turn + 1) * time_step))
        efield = efield.at[0].add(time_step * signal * source_term)
        slabs.append(efield[:, :, :, Z0 : Z0 + slab_depth])
        monitors.append(jnp.sum(efield * monitor_pick, axis=3, keepdims=True))
    total = jnp.zeros((efield.shape[1], efield.shape[2], slab_depth), jnp.float32)
    for turn in range(STEPS):
        adj_h = adj_h - time_step * curl(adj_e, True)
        adj_e = adj_e + coef * curl(adj_h, False)
        adj_e = adj_e + 2.0 * time_step * monitors[STEPS - 1 - turn] * monitor_mask
        total = total + jnp.sum(
            slabs[STEPS - 1 - turn] * adj_e[:, :, :, Z0 : Z0 + slab_depth], axis=0
        )
    return (efield, adj_e, total)


def per_device(
    forward_efield,
    forward_hfield,
    adjoint_efield,
    adjoint_hfield,
    background,
    design,
    source_profile,
    source_layer,
    monitor_layer,
):
    groups = lax.axis_size("wl")
    owned = design.shape[0]
    slab_depth = owned * groups
    depth = background.shape[2]
    tiles = lax.all_gather(design, "wl", axis=0, tiled=True)
    permit = jnp.concatenate(
        [
            background[:, :, :Z0],
            jnp.transpose(tiles, (1, 2, 0)),
            background[:, :, Z0 + slab_depth :],
        ],
        axis=2,
    )
    layers = lax.iota(jnp.int32, depth)
    wave_index = lax.axis_index("wl").astype(jnp.float32)
    omega = jnp.float32(2.0 * math.pi) / (16.0 + 32.0 * wave_index / groups)
    source_mask = (layers == source_layer[0]).astype(jnp.float32)
    monitor_mask = (layers == monitor_layer[0]).astype(jnp.float32)
    source_term = source_profile[0][:, :, None] * source_mask
    coef = time_step / permit
    efield, adj_e, total = run_window(
        forward_efield[0],
        forward_hfield[0],
        adjoint_efield[0],
        adjoint_hfield[0],
        coef,
        source_term,
        omega,
        monitor_mask,
        slab_depth,
    )
    local_grad = jnp.transpose(omega * omega * total, (2, 0, 1))
    summed = lax.psum(local_grad, "wl")
    gradient = lax.dynamic_slice_in_dim(summed, lax.axis_index("wl") * owned, owned, 0)
    return (efield[None], adj_e[None], gradient)


def solution(mesh):
    return jax.shard_map(
        per_device,
        mesh=mesh,
        in_specs=(
            P("wl", None, "gx", "gy", None),
            P("wl", None, "gx", "gy", None),
            P("wl", None, "gx", "gy", None),
            P("wl", None, "gx", "gy", None),
            P("gx", "gy", None),
            P("wl", "gx", "gy"),
            P("wl", "gx", "gy"),
            P("wl"),
            P("wl"),
        ),
        out_specs=(
            P("wl", None, "gx", "gy", None),
            P("wl", None, "gx", "gy", None),
            P("wl", "gx", "gy"),
        ),
        check_vma=False,
    )
```

profile of v0, /device:TPU:0, one launch (start us, length us, event | category | flops | bytes accessed | tf_op | source)
XLA Modules:
  0.0 120.3 jit_solution(9037135590626028653)
XLA Ops:
  0.6 1.0 slice.645
  1.7 1.3 %collective-permute-start = (f32[3,32,1,128]{3,2,1,0:T(1,128)S(1)}, f32[3,32,1,128]{3,2,1,0:T(1,128)S(1)}, u32[]{:S(2)}, u32[]{:S(2)}) collective-permute-start(f32[3,32,1,128]{3,2,1,0:T(1,128)S(1)} %slice.645), channel_id=1, source_target_pairs={{1,0},{2,1},{3,2},{5,4},{6,5},{7,6},{9,8},{10,9},{11,10},{13,12},{... | collective-permute-start | bytes 147464 | tf_op jit(solution)/shard_map/ppermute | solution.py:15
  3.0 0.7 slice.651
  3.7 1.3 %collective-permute-start.1 = (f32[3,1,8,128]{3,2,1,0:T(8,128)S(1)}, f32[3,1,8,128]{3,2,1,0:T(8,128)S(1)}, u32[]{:S(2)}, u32[]{:S(2)}) collective-permute-start(f32[3,1,8,128]{3,2,1,0:T(8,128)S(1)} %slice.651), channel_id=1, source_target_pairs={{4,0},{5,1},{6,2},{7,3},{12,8},{13,9},{14,10},{15,11},{20,16},{21,... | collective-permute-start | bytes 36872 | tf_op jit(solution)/shard_map/ppermute | solution.py:15
  5.0 1.0 slice.714
  6.0 1.4 %collective-permute-start.12 = (f32[3,32,1,128]{3,2,1,0:T(1,128)S(1)}, f32[3,32,1,128]{3,2,1,0:T(1,128)S(1)}, u32[]{:S(2)}, u32[]{:S(2)}) collective-permute-start(f32[3,32,1,128]{3,2,1,0:T(1,128)S(1)} %slice.714), channel_id=1, source_target_pairs={{1,0},{2,1},{3,2},{5,4},{6,5},{7,6},{9,8},{10,9},{11,10},{13,12},{... | collective-permute-start | bytes 147464 | tf_op jit(solution)/shard_map/ppermute | solution.py:15
  7.4 0.7 slice.720
  8.2 1.3 %collective-permute-start.13 = (f32[3,1,8,128]{3,2,1,0:T(8,128)S(1)}, f32[3,1,8,128]{3,2,1,0:T(8,128)S(1)}, u32[]{:S(2)}, u32[]{:S(2)}) collective-permute-start(f32[3,1,8,128]{3,2,1,0:T(8,128)S(1)} %slice.720), channel_id=1, source_target_pairs={{4,0},{5,1},{6,2},{7,3},{12,8},{13,9},{14,10},{15,11},{20,16},{21,... | collective-permute-start | bytes 36872 | tf_op jit(solution)/shard_map/ppermute | solution.py:15
  9.5 6.2 %all_gather.3 = f32[8,32,8]{1,2,0:T(8,128)S(1)} all-gather(f32[2,32,8]{1,2,0:T(8,128)S(1)} %copy-done.26), channel_id=1, replica_groups=mesh['wl'=4,'gx'=2,'gy'=4] {'wl'}, dimensions={0}, use_global_device_ids=true | all-gather | bytes 10240 | tf_op jit(solution)/shard_map/all_gather | solution.py:83
  17.6 1.0 copy-done
  20.1 0.9 copy-done.1
  21.1 5.2 %collective-permute-start.2 = (f32[3,32,1,128]{3,2,1,0:T(1,128)S(1)}, f32[3,32,1,128]{3,2,1,0:T(1,128)S(1)}, u32[]{:S(2)}, u32[]{:S(2)}) collective-permute-start(f32[3,32,1,128]{3,2,1,0:T(1,128)S(1)} %slice.655), channel_id=1, source_target_pairs={{0,1},{1,2},{2,3},{4,5},{5,6},{6,7},{8,9},{9,10},{10,11},{12,13},{... | collective-permute-start | bytes 147464 | tf_op jit(solution)/shard_map/ppermute | solution.py:15
  26.3 4.5 %collective-permute-start.3 = (f32[3,1,8,128]{3,2,1,0:T(8,128)S(1)}, f32[3,1,8,128]{3,2,1,0:T(8,128)S(1)}, u32[]{:S(2)}, u32[]{:S(2)}) collective-permute-start(f32[3,1,8,128]{3,2,1,0:T(8,128)S(1)} %slice.661), channel_id=1, source_target_pairs={{0,4},{1,5},{2,6},{3,7},{8,12},{9,13},{10,14},{11,15},{16,20},{17,... | collective-permute-start | bytes 36872 | tf_op jit(solution)/shard_map/ppermute | solution.py:15
  31.1 1.2 collective-permute-done.3
  32.7 1.3 %collective-permute-start.4 = (f32[3,32,1,128]{3,2,1,0:T(1,128)S(1)}, f32[3,32,1,128]{3,2,1,0:T(1,128)S(1)}, u32[]{:S(2)}, u32[]{:S(2)}) collective-permute-start(f32[3,32,1,128]{3,2,1,0:T(1,128)S(1)} %slice.668), channel_id=1, source_target_pairs={{1,0},{2,1},{3,2},{5,4},{6,5},{7,6},{9,8},{10,9},{11,10},{13,12},{... | collective-permute-start | bytes 147464 | tf_op jit(solution)/shard_map/ppermute | solution.py:15
  34.0 1.3 %collective-permute-start.5 = (f32[3,1,8,128]{3,2,1,0:T(8,128)S(1)}, f32[3,1,8,128]{3,2,1,0:T(8,128)S(1)}, u32[]{:S(2)}, u32[]{:S(2)}) collective-permute-start(f32[3,1,8,128]{3,2,1,0:T(8,128)S(1)} %slice.674), channel_id=1, source_target_pairs={{4,0},{5,1},{6,2},{7,3},{12,8},{13,9},{14,10},{15,11},{20,16},{21,... | collective-permute-start | bytes 36872 | tf_op jit(solution)/shard_map/ppermute | solution.py:15
  35.6 4.0 %collective-permute-done.5 = f32[3,1,8,128]{3,2,1,0:T(8,128)S(1)} collective-permute-done((f32[3,1,8,128]{3,2,1,0:T(8,128)S(1)}, f32[3,1,8,128]{3,2,1,0:T(8,128)S(1)}, u32[]{:S(2)}, u32[]{:S(2)}) %collective-permute-start.5) | collective-permute-done | bytes 12320 | tf_op jit(solution)/shard_map/ppermute | solution.py:15
  40.0 4.6 %collective-permute-start.6 = (f32[3,32,1,128]{3,2,1,0:T(1,128)S(1)}, f32[3,32,1,128]{3,2,1,0:T(1,128)S(1)}, u32[]{:S(2)}, u32[]{:S(2)}) collective-permute-start(f32[3,32,1,128]{3,2,1,0:T(1,128)S(1)} %slice.678), channel_id=1, source_target_pairs={{0,1},{1,2},{2,3},{4,5},{5,6},{6,7},{8,9},{9,10},{10,11},{12,13},{... | collective-permute-start | bytes 147464 | tf_op jit(solution)/shard_map/ppermute | solution.py:15
  44.5 2.7 %collective-permute-start.7 = (f32[3,1,8,128]{3,2,1,0:T(8,128)S(1)}, f32[3,1,8,128]{3,2,1,0:T(8,128)S(1)}, u32[]{:S(2)}, u32[]{:S(2)}) collective-permute-start(f32[3,1,8,128]{3,2,1,0:T(8,128)S(1)} %slice.684), channel_id=1, source_target_pairs={{0,4},{1,5},{2,6},{3,7},{8,12},{9,13},{10,14},{11,15},{16,20},{17,... | collective-permute-start | bytes 36872 | tf_op jit(solution)/shard_map/ppermute | solution.py:15
  47.4 3.9 %collective-permute-start.14 = (f32[3,32,1,128]{3,2,1,0:T(1,128)S(1)}, f32[3,32,1,128]{3,2,1,0:T(1,128)S(1)}, u32[]{:S(2)}, u32[]{:S(2)}) collective-permute-start(f32[3,32,1,128]{3,2,1,0:T(1,128)S(1)} %slice.724), channel_id=1, source_target_pairs={{0,1},{1,2},{2,3},{4,5},{5,6},{6,7},{8,9},{9,10},{10,11},{12,13},{... | collective-permute-start | bytes 147464 | tf_op jit(solution)/shard_map/ppermute | solution.py:15
  51.3 1.3 %collective-permute-start.15 = (f32[3,1,8,128]{3,2,1,0:T(8,128)S(1)}, f32[3,1,8,128]{3,2,1,0:T(8,128)S(1)}, u32[]{:S(2)}, u32[]{:S(2)}) collective-permute-start(f32[3,1,8,128]{3,2,1,0:T(8,128)S(1)} %slice.730), channel_id=1, source_target_pairs={{0,4},{1,5},{2,6},{3,7},{8,12},{9,13},{10,14},{11,15},{16,20},{17,... | collective-permute-start | bytes 36872 | tf_op jit(solution)/shard_map/ppermute | solution.py:15
  53.1 1.3 %collective-permute-start.8 = (f32[3,32,1,128]{3,2,1,0:T(1,128)S(1)}, f32[3,32,1,128]{3,2,1,0:T(1,128)S(1)}, u32[]{:S(2)}, u32[]{:S(2)}) collective-permute-start(f32[3,32,1,128]{3,2,1,0:T(1,128)S(1)} %slice.691), channel_id=1, source_target_pairs={{1,0},{2,1},{3,2},{5,4},{6,5},{7,6},{9,8},{10,9},{11,10},{13,12},{... | collective-permute-start | bytes 147464 | tf_op jit(solution)/shard_map/ppermute | solution.py:15
  54.4 1.3 %collective-permute-start.9 = (f32[3,1,8,128]{3,2,1,0:T(8,128)S(1)}, f32[3,1,8,128]{3,2,1,0:T(8,128)S(1)}, u32[]{:S(2)}, u32[]{:S(2)}) collective-permute-start(f32[3,1,8,128]{3,2,1,0:T(8,128)S(1)} %slice.697), channel_id=1, source_target_pairs={{4,0},{5,1},{6,2},{7,3},{12,8},{13,9},{14,10},{15,11},{20,16},{21,... | collective-permute-start | bytes 36872 | tf_op jit(solution)/shard_map/ppermute | solution.py:15
  56.2 3.8 %collective-permute-done.9 = f32[3,1,8,128]{3,2,1,0:T(8,128)S(1)} collective-permute-done((f32[3,1,8,128]{3,2,1,0:T(8,128)S(1)}, f32[3,1,8,128]{3,2,1,0:T(8,128)S(1)}, u32[]{:S(2)}, u32[]{:S(2)}) %collective-permute-start.9) | collective-permute-done | bytes 12320 | tf_op jit(solution)/shard_map/ppermute | solution.py:15
  60.4 4.5 %collective-permute-start.10 = (f32[3,32,1,128]{3,2,1,0:T(1,128)S(1)}, f32[3,32,1,128]{3,2,1,0:T(1,128)S(1)}, u32[]{:S(2)}, u32[]{:S(2)}) collective-permute-start(f32[3,32,1,128]{3,2,1,0:T(1,128)S(1)} %slice.701), channel_id=1, source_target_pairs={{0,1},{1,2},{2,3},{4,5},{5,6},{6,7},{8,9},{9,10},{10,11},{12,13},{... | collective-permute-start | bytes 147464 | tf_op jit(solution)/shard_map/ppermute | solution.py:15
  64.9 1.6 %collective-permute-start.11 = (f32[3,1,8,128]{3,2,1,0:T(8,128)S(1)}, f32[3,1,8,128]{3,2,1,0:T(8,128)S(1)}, u32[]{:S(2)}, u32[]{:S(2)}) collective-permute-start(f32[3,1,8,128]{3,2,1,0:T(8,128)S(1)} %slice.707), channel_id=1, source_target_pairs={{0,4},{1,5},{2,6},{3,7},{8,12},{9,13},{10,14},{11,15},{16,20},{17,... | collective-permute-start | bytes 36872 | tf_op jit(solution)/shard_map/ppermute | solution.py:15
  66.7 1.3 %collective-permute-done.11 = f32[3,1,8,128]{3,2,1,0:T(8,128)S(1)} collective-permute-done((f32[3,1,8,128]{3,2,1,0:T(8,128)S(1)}, f32[3,1,8,128]{3,2,1,0:T(8,128)S(1)}, u32[]{:S(2)}, u32[]{:S(2)}) %collective-permute-start.11) | collective-permute-done | bytes 12320 | tf_op jit(solution)/shard_map/ppermute | solution.py:15
  68.5 0.8 multiply_reduce_fusion
  69.5 1.3 %collective-permute-start.16 = (f32[3,32,1,128]{3,2,1,0:T(1,128)S(1)}, f32[3,32,1,128]{3,2,1,0:T(1,128)S(1)}, u32[]{:S(2)}, u32[]{:S(2)}) collective-permute-start(f32[3,32,1,128]{3,2,1,0:T(1,128)S(1)} %slice.736), channel_id=1, source_target_pairs={{1,0},{2,1},{3,2},{5,4},{6,5},{7,6},{9,8},{10,9},{11,10},{13,12},{... | collective-permute-start | bytes 147464 | tf_op jit(solution)/shard_map/ppermute | solution.py:15
  70.8 1.3 %collective-permute-start.17 = (f32[3,1,8,128]{3,2,1,0:T(8,128)S(1)}, f32[3,1,8,128]{3,2,1,0:T(8,128)S(1)}, u32[]{:S(2)}, u32[]{:S(2)}) collective-permute-start(f32[3,1,8,128]{3,2,1,0:T(8,128)S(1)} %slice.742), channel_id=1, source_target_pairs={{4,0},{5,1},{6,2},{7,3},{12,8},{13,9},{14,10},{15,11},{20,16},{21,... | collective-permute-start | bytes 36872 | tf_op jit(solution)/shard_map/ppermute | solution.py:15
  72.4 4.0 %collective-permute-done.17 = f32[3,1,8,128]{3,2,1,0:T(8,128)S(1)} collective-permute-done((f32[3,1,8,128]{3,2,1,0:T(8,128)S(1)}, f32[3,1,8,128]{3,2,1,0:T(8,128)S(1)}, u32[]{:S(2)}, u32[]{:S(2)}) %collective-permute-start.17) | collective-permute-done | bytes 12320 | tf_op jit(solution)/shard_map/ppermute | solution.py:15
  76.9 4.5 %collective-permute-start.18 = (f32[3,32,1,128]{3,2,1,0:T(1,128)S(1)}, f32[3,32,1,128]{3,2,1,0:T(1,128)S(1)}, u32[]{:S(2)}, u32[]{:S(2)}) collective-permute-start(f32[3,32,1,128]{3,2,1,0:T(1,128)S(1)} %slice.746), channel_id=1, source_target_pairs={{0,1},{1,2},{2,3},{4,5},{5,6},{6,7},{8,9},{9,10},{10,11},{12,13},{... | collective-permute-start | bytes 147464 | tf_op jit(solution)/shard_map/ppermute | solution.py:15
  81.4 1.6 %collective-permute-start.19 = (f32[3,1,8,128]{3,2,1,0:T(8,128)S(1)}, f32[3,1,8,128]{3,2,1,0:T(8,128)S(1)}, u32[]{:S(2)}, u32[]{:S(2)}) collective-permute-start(f32[3,1,8,128]{3,2,1,0:T(8,128)S(1)} %slice.752), channel_id=1, source_target_pairs={{0,4},{1,5},{2,6},{3,7},{8,12},{9,13},{10,14},{11,15},{16,20},{17,... | collective-permute-start | bytes 36872 | tf_op jit(solution)/shard_map/ppermute | solution.py:15
  83.1 1.4 %collective-permute-done.19 = f32[3,1,8,128]{3,2,1,0:T(8,128)S(1)} collective-permute-done((f32[3,1,8,128]{3,2,1,0:T(8,128)S(1)}, f32[3,1,8,128]{3,2,1,0:T(8,128)S(1)}, u32[]{:S(2)}, u32[]{:S(2)}) %collective-permute-start.19) | collective-permute-done | bytes 12320 | tf_op jit(solution)/shard_map/ppermute | solution.py:15
  85.5 0.6 slice.758
  86.1 1.3 %collective-permute-start.20 = (f32[3,32,1,128]{3,2,1,0:T(1,128)}, f32[3,32,1,128]{3,2,1,0:T(1,128)}, u32[]{:S(2)}, u32[]{:S(2)}) collective-permute-start(f32[3,32,1,128]{3,2,1,0:T(1,128)} %slice.758), channel_id=1, source_target_pairs={{1,0},{2,1},{3,2},{5,4},{6,5},{7,6},{9,8},{10,9},{11,10},{13,12},{... | collective-permute-start | bytes 147464 | tf_op jit(solution)/shard_map/ppermute | solution.py:15
  87.4 1.3 %collective-permute-start.21 = (f32[3,1,8,128]{3,2,1,0:T(8,128)S(1)}, f32[3,1,8,128]{3,2,1,0:T(8,128)}, u32[]{:S(2)}, u32[]{:S(2)}) collective-permute-start(f32[3,1,8,128]{3,2,1,0:T(8,128)S(1)} %slice.764), channel_id=1, source_target_pairs={{4,0},{5,1},{6,2},{7,3},{12,8},{13,9},{14,10},{15,11},{20,16},{21,... | collective-permute-start | bytes 36872 | tf_op jit(solution)/shard_map/ppermute | solution.py:15
  88.7 0.8 slice.784
  90.4 2.8 %collective-permute-done.21 = f32[3,1,8,128]{3,2,1,0:T(8,128)} collective-permute-done((f32[3,1,8,128]{3,2,1,0:T(8,128)S(1)}, f32[3,1,8,128]{3,2,1,0:T(8,128)}, u32[]{:S(2)}, u32[]{:S(2)}) %collective-permute-start.21) | collective-permute-done | bytes 12320 | tf_op jit(solution)/shard_map/ppermute | solution.py:15
  93.2 1.2 pad_subtract_fusion.1
  94.4 0.8 copy-done.7
  95.4 4.5 %collective-permute-start.22 = (f32[3,32,1,128]{3,2,1,0:T(1,128)S(1)}, f32[3,32,1,128]{3,2,1,0:T(1,128)S(1)}, u32[]{:S(2)}, u32[]{:S(2)}) collective-permute-start(f32[3,32,1,128]{3,2,1,0:T(1,128)S(1)} %slice.768), channel_id=1, source_target_pairs={{0,1},{1,2},{2,3},{4,5},{5,6},{6,7},{8,9},{9,10},{10,11},{12,13},{... | collective-permute-start | bytes 147464 | tf_op jit(solution)/shard_map/ppermute | solution.py:15
  100.0 3.3 %collective-permute-start.23 = (f32[3,1,8,128]{3,2,1,0:T(8,128)S(1)}, f32[3,1,8,128]{3,2,1,0:T(8,128)S(1)}, u32[]{:S(2)}, u32[]{:S(2)}) collective-permute-start(f32[3,1,8,128]{3,2,1,0:T(8,128)S(1)} %slice.774), channel_id=1, source_target_pairs={{0,4},{1,5},{2,6},{3,7},{8,12},{9,13},{10,14},{11,15},{16,20},{17,... | collective-permute-start | bytes 36872 | tf_op jit(solution)/shard_map/ppermute | solution.py:15
  103.6 1.1 collective-permute-done.23
  105.0 0.8 copy-done.23
  106.5 11.6 %psum.7 = f32[8,32,8]{0,2,1:T(8,128)S(1)} all-reduce(f32[8,32,8]{0,2,1:T(8,128)S(1)} %multiply_bitcast_fusion), channel_id=1, replica_groups=mesh['wl'=4,'gx'=2,'gy'=4] {'wl'}, use_global_device_ids=true, to_apply=%region_6.0 | all-reduce | flops 2048 | bytes 16384 | tf_op jit(solution)/shard_map/psum | solution.py:111
  118.2 0.7 copy.16
  119.1 1.1 fusion.19
  (161 shorter events, 9.4 us)
Async XLA Ops:
  1.7 18.2 %collective-permute-start = (f32[3,32,1,128]{3,2,1,0:T(1,128)S(1)}, f32[3,32,1,128]{3,2,1,0:T(1,128)S(1)}, u32[]{:S(2)}, u32[]{:S(2)}) collective-permute-start(f32[3,32,1,128]{3,2,1,0:T(1,128)S(1)} %slice.645), channel_id=1, source_target_pairs={{1,0},{2,1},{3,2},{5,4},{6,5},{7,6},{9,8},{10,9},{11,10},{13,12},{... | collective-permute-start | bytes 147464 | tf_op jit(solution)/shard_map/ppermute | solution.py:15
  3.7 16.2 %collective-permute-start.1 = (f32[3,1,8,128]{3,2,1,0:T(8,128)S(1)}, f32[3,1,8,128]{3,2,1,0:T(8,128)S(1)}, u32[]{:S(2)}, u32[]{:S(2)}) collective-permute-start(f32[3,1,8,128]{3,2,1,0:T(8,128)S(1)} %slice.651), channel_id=1, source_target_pairs={{4,0},{5,1},{6,2},{7,3},{12,8},{13,9},{14,10},{15,11},{20,16},{21,... | collective-permute-start | bytes 36872 | tf_op jit(solution)/shard_map/ppermute | solution.py:15
  5.0 4.5 %copy-start.26 = (f32[2,32,8]{1,2,0:T(8,128)S(1)}, f32[2,32,8]{1,2,0:T(8,128)}, u32[]{:S(2)}) copy-start(f32[2,32,8]{1,2,0:T(8,128)} %param.20) | copy-start | bytes 6148
  6.0 9.8 %copy-start.24 = (f32[32,8,128]{2,1,0:T(8,128)S(1)}, f32[32,8,128]{2,1,0:T(8,128)}, u32[]{:S(2)}) copy-start(f32[32,8,128]{2,1,0:T(8,128)} %param.19) | copy-start | bytes 393220
  6.0 24.9 %collective-permute-start.12 = (f32[3,32,1,128]{3,2,1,0:T(1,128)S(1)}, f32[3,32,1,128]{3,2,1,0:T(1,128)S(1)}, u32[]{:S(2)}, u32[]{:S(2)}) collective-permute-start(f32[3,32,1,128]{3,2,1,0:T(1,128)S(1)} %slice.714), channel_id=1, source_target_pairs={{1,0},{2,1},{3,2},{5,4},{6,5},{7,6},{9,8},{10,9},{11,10},{13,12},{... | collective-permute-start | bytes 147464 | tf_op jit(solution)/shard_map/ppermute | solution.py:15
  8.2 22.7 %collective-permute-start.13 = (f32[3,1,8,128]{3,2,1,0:T(8,128)S(1)}, f32[3,1,8,128]{3,2,1,0:T(8,128)S(1)}, u32[]{:S(2)}, u32[]{:S(2)}) collective-permute-start(f32[3,1,8,128]{3,2,1,0:T(8,128)S(1)} %slice.720), channel_id=1, source_target_pairs={{4,0},{5,1},{6,2},{7,3},{12,8},{13,9},{14,10},{15,11},{20,16},{21,... | collective-permute-start | bytes 36872 | tf_op jit(solution)/shard_map/ppermute | solution.py:15
  15.8 1.6 %copy-start.3 = (f32[1,3,32,8,128]{4,3,2,1,0:T(8,128)S(1)}, f32[1,3,32,8,128]{4,3,2,1,0:T(8,128)}, u32[]{:S(2)}) copy-start(f32[1,3,32,8,128]{4,3,2,1,0:T(8,128)} %param.15) | copy-start | bytes 1179652
  17.6 1.0 copy-start
  20.0 1.0 copy-start.1
  21.1 11.2 %collective-permute-start.2 = (f32[3,32,1,128]{3,2,1,0:T(1,128)S(1)}, f32[3,32,1,128]{3,2,1,0:T(1,128)S(1)}, u32[]{:S(2)}, u32[]{:S(2)}) collective-permute-start(f32[3,32,1,128]{3,2,1,0:T(1,128)S(1)} %slice.655), channel_id=1, source_target_pairs={{0,1},{1,2},{2,3},{4,5},{5,6},{6,7},{8,9},{9,10},{10,11},{12,13},{... | collective-permute-start | bytes 147464 | tf_op jit(solution)/shard_map/ppermute | solution.py:15
  26.3 5.9 %collective-permute-start.3 = (f32[3,1,8,128]{3,2,1,0:T(8,128)S(1)}, f32[3,1,8,128]{3,2,1,0:T(8,128)S(1)}, u32[]{:S(2)}, u32[]{:S(2)}) collective-permute-start(f32[3,1,8,128]{3,2,1,0:T(8,128)S(1)} %slice.661), channel_id=1, source_target_pairs={{0,4},{1,5},{2,6},{3,7},{8,12},{9,13},{10,14},{11,15},{16,20},{17,... | collective-permute-start | bytes 36872 | tf_op jit(solution)/shard_map/ppermute | solution.py:15
  32.7 6.9 %collective-permute-start.4 = (f32[3,32,1,128]{3,2,1,0:T(1,128)S(1)}, f32[3,32,1,128]{3,2,1,0:T(1,128)S(1)}, u32[]{:S(2)}, u32[]{:S(2)}) collective-permute-start(f32[3,32,1,128]{3,2,1,0:T(1,128)S(1)} %slice.668), channel_id=1, source_target_pairs={{1,0},{2,1},{3,2},{5,4},{6,5},{7,6},{9,8},{10,9},{11,10},{13,12},{... | collective-permute-start | bytes 147464 | tf_op jit(solution)/shard_map/ppermute | solution.py:15
  34.0 5.6 %collective-permute-start.5 = (f32[3,1,8,128]{3,2,1,0:T(8,128)S(1)}, f32[3,1,8,128]{3,2,1,0:T(8,128)S(1)}, u32[]{:S(2)}, u32[]{:S(2)}) collective-permute-start(f32[3,1,8,128]{3,2,1,0:T(8,128)S(1)} %slice.674), channel_id=1, source_target_pairs={{4,0},{5,1},{6,2},{7,3},{12,8},{13,9},{14,10},{15,11},{20,16},{21,... | collective-permute-start | bytes 36872 | tf_op jit(solution)/shard_map/ppermute | solution.py:15
  39.8 7.4 %copy-start.2 = (f32[1,3,32,8,128]{4,3,2,1,0:T(8,128)S(1)}, f32[1,3,32,8,128]{4,3,2,1,0:T(8,128)}, u32[]{:S(2)}) copy-start(f32[1,3,32,8,128]{4,3,2,1,0:T(8,128)} %param.18) | copy-start | bytes 1179652
  40.0 12.7 %collective-permute-start.6 = (f32[3,32,1,128]{3,2,1,0:T(1,128)S(1)}, f32[3,32,1,128]{3,2,1,0:T(1,128)S(1)}, u32[]{:S(2)}, u32[]{:S(2)}) collective-permute-start(f32[3,32,1,128]{3,2,1,0:T(1,128)S(1)} %slice.678), channel_id=1, source_target_pairs={{0,1},{1,2},{2,3},{4,5},{5,6},{6,7},{8,9},{9,10},{10,11},{12,13},{... | collective-permute-start | bytes 147464 | tf_op jit(solution)/shard_map/ppermute | solution.py:15
  44.5 8.1 %collective-permute-start.7 = (f32[3,1,8,128]{3,2,1,0:T(8,128)S(1)}, f32[3,1,8,128]{3,2,1,0:T(8,128)S(1)}, u32[]{:S(2)}, u32[]{:S(2)}) collective-permute-start(f32[3,1,8,128]{3,2,1,0:T(8,128)S(1)} %slice.684), channel_id=1, source_target_pairs={{0,4},{1,5},{2,6},{3,7},{8,12},{9,13},{10,14},{11,15},{16,20},{17,... | collective-permute-start | bytes 36872 | tf_op jit(solution)/shard_map/ppermute | solution.py:15
  47.4 8.4 %collective-permute-start.14 = (f32[3,32,1,128]{3,2,1,0:T(1,128)S(1)}, f32[3,32,1,128]{3,2,1,0:T(1,128)S(1)}, u32[]{:S(2)}, u32[]{:S(2)}) collective-permute-start(f32[3,32,1,128]{3,2,1,0:T(1,128)S(1)} %slice.724), channel_id=1, source_target_pairs={{0,1},{1,2},{2,3},{4,5},{5,6},{6,7},{8,9},{9,10},{10,11},{12,13},{... | collective-permute-start | bytes 147464 | tf_op jit(solution)/shard_map/ppermute | solution.py:15
  51.3 4.5 %collective-permute-start.15 = (f32[3,1,8,128]{3,2,1,0:T(8,128)S(1)}, f32[3,1,8,128]{3,2,1,0:T(8,128)S(1)}, u32[]{:S(2)}, u32[]{:S(2)}) collective-permute-start(f32[3,1,8,128]{3,2,1,0:T(8,128)S(1)} %slice.730), channel_id=1, source_target_pairs={{0,4},{1,5},{2,6},{3,7},{8,12},{9,13},{10,14},{11,15},{16,20},{17,... | collective-permute-start | bytes 36872 | tf_op jit(solution)/shard_map/ppermute | solution.py:15
  53.1 6.9 %collective-permute-start.8 = (f32[3,32,1,128]{3,2,1,0:T(1,128)S(1)}, f32[3,32,1,128]{3,2,1,0:T(1,128)S(1)}, u32[]{:S(2)}, u32[]{:S(2)}) collective-permute-start(f32[3,32,1,128]{3,2,1,0:T(1,128)S(1)} %slice.691), channel_id=1, source_target_pairs={{1,0},{2,1},{3,2},{5,4},{6,5},{7,6},{9,8},{10,9},{11,10},{13,12},{... | collective-permute-start | bytes 147464 | tf_op jit(solution)/shard_map/ppermute | solution.py:15
  54.4 5.6 %collective-permute-start.9 = (f32[3,1,8,128]{3,2,1,0:T(8,128)S(1)}, f32[3,1,8,128]{3,2,1,0:T(8,128)S(1)}, u32[]{:S(2)}, u32[]{:S(2)}) collective-permute-start(f32[3,1,8,128]{3,2,1,0:T(8,128)S(1)} %slice.697), channel_id=1, source_target_pairs={{4,0},{5,1},{6,2},{7,3},{12,8},{13,9},{14,10},{15,11},{20,16},{21,... | collective-permute-start | bytes 36872 | tf_op jit(solution)/shard_map/ppermute | solution.py:15
  60.4 7.6 %collective-permute-start.10 = (f32[3,32,1,128]{3,2,1,0:T(1,128)S(1)}, f32[3,32,1,128]{3,2,1,0:T(1,128)S(1)}, u32[]{:S(2)}, u32[]{:S(2)}) collective-permute-start(f32[3,32,1,128]{3,2,1,0:T(1,128)S(1)} %slice.701), channel_id=1, source_target_pairs={{0,1},{1,2},{2,3},{4,5},{5,6},{6,7},{8,9},{9,10},{10,11},{12,13},{... | collective-permute-start | bytes 147464 | tf_op jit(solution)/shard_map/ppermute | solution.py:15
  64.9 3.0 %collective-permute-start.11 = (f32[3,1,8,128]{3,2,1,0:T(8,128)S(1)}, f32[3,1,8,128]{3,2,1,0:T(8,128)S(1)}, u32[]{:S(2)}, u32[]{:S(2)}) collective-permute-start(f32[3,1,8,128]{3,2,1,0:T(8,128)S(1)} %slice.707), channel_id=1, source_target_pairs={{0,4},{1,5},{2,6},{3,7},{8,12},{9,13},{10,14},{11,15},{16,20},{17,... | collective-permute-start | bytes 36872 | tf_op jit(solution)/shard_map/ppermute | solution.py:15
  69.3 15.5 %copy-start.17 = (f32[3,32,8]{2,1,0:T(8,128)}, f32[3,32,8]{2,1,0:T(8,128)S(1)}, u32[]{:S(2)}) copy-start(f32[3,32,8]{2,1,0:T(8,128)S(1)} %get-tuple-element.46) | copy-start | bytes 9220
  69.3 15.5 %copy-start.20 = (f32[3,32,8]{2,1,0:T(8,128)}, f32[3,32,8]{2,1,0:T(8,128)S(1)}, u32[]{:S(2)}) copy-start(f32[3,32,8]{2,1,0:T(8,128)S(1)} %get-tuple-element.45) | copy-start | bytes 9220
  69.5 6.9 %collective-permute-start.16 = (f32[3,32,1,128]{3,2,1,0:T(1,128)S(1)}, f32[3,32,1,128]{3,2,1,0:T(1,128)S(1)}, u32[]{:S(2)}, u32[]{:S(2)}) collective-permute-start(f32[3,32,1,128]{3,2,1,0:T(1,128)S(1)} %slice.736), channel_id=1, source_target_pairs={{1,0},{2,1},{3,2},{5,4},{6,5},{7,6},{9,8},{10,9},{11,10},{13,12},{... | collective-permute-start | bytes 147464 | tf_op jit(solution)/shard_map/ppermute | solution.py:15
  70.8 5.6 %collective-permute-start.17 = (f32[3,1,8,128]{3,2,1,0:T(8,128)S(1)}, f32[3,1,8,128]{3,2,1,0:T(8,128)S(1)}, u32[]{:S(2)}, u32[]{:S(2)}) collective-permute-start(f32[3,1,8,128]{3,2,1,0:T(8,128)S(1)} %slice.742), channel_id=1, source_target_pairs={{4,0},{5,1},{6,2},{7,3},{12,8},{13,9},{14,10},{15,11},{20,16},{21,... | collective-permute-start | bytes 36872 | tf_op jit(solution)/shard_map/ppermute | solution.py:15
  76.7 7.7 %copy-start.6 = (f32[1,32,8,128]{3,2,1,0:T(8,128)}, f32[1,32,8,128]{3,2,1,0:T(8,128)S(1)}, u32[]{:S(2)}) copy-start(f32[1,32,8,128]{3,2,1,0:T(8,128)S(1)} %get-tuple-element.67) | copy-start | bytes 393220
  76.9 7.6 %collective-permute-start.18 = (f32[3,32,1,128]{3,2,1,0:T(1,128)S(1)}, f32[3,32,1,128]{3,2,1,0:T(1,128)S(1)}, u32[]{:S(2)}, u32[]{:S(2)}) collective-permute-start(f32[3,32,1,128]{3,2,1,0:T(1,128)S(1)} %slice.746), channel_id=1, source_target_pairs={{0,1},{1,2},{2,3},{4,5},{5,6},{6,7},{8,9},{9,10},{10,11},{12,13},{... | collective-permute-start | bytes 147464 | tf_op jit(solution)/shard_map/ppermute | solution.py:15
  81.4 3.0 %collective-permute-start.19 = (f32[3,1,8,128]{3,2,1,0:T(8,128)S(1)}, f32[3,1,8,128]{3,2,1,0:T(8,128)S(1)}, u32[]{:S(2)}, u32[]{:S(2)}) collective-permute-start(f32[3,1,8,128]{3,2,1,0:T(8,128)S(1)} %slice.752), channel_id=1, source_target_pairs={{0,4},{1,5},{2,6},{3,7},{8,12},{9,13},{10,14},{11,15},{16,20},{17,... | collective-permute-start | bytes 36872 | tf_op jit(solution)/shard_map/ppermute | solution.py:15
  86.1 7.0 %collective-permute-start.20 = (f32[3,32,1,128]{3,2,1,0:T(1,128)}, f32[3,32,1,128]{3,2,1,0:T(1,128)}, u32[]{:S(2)}, u32[]{:S(2)}) collective-permute-start(f32[3,32,1,128]{3,2,1,0:T(1,128)} %slice.758), channel_id=1, source_target_pairs={{1,0},{2,1},{3,2},{5,4},{6,5},{7,6},{9,8},{10,9},{11,10},{13,12},{... | collective-permute-start | bytes 147464 | tf_op jit(solution)/shard_map/ppermute | solution.py:15
  87.4 5.7 %collective-permute-start.21 = (f32[3,1,8,128]{3,2,1,0:T(8,128)S(1)}, f32[3,1,8,128]{3,2,1,0:T(8,128)}, u32[]{:S(2)}, u32[]{:S(2)}) collective-permute-start(f32[3,1,8,128]{3,2,1,0:T(8,128)S(1)} %slice.764), channel_id=1, source_target_pairs={{4,0},{5,1},{6,2},{7,3},{12,8},{13,9},{14,10},{15,11},{20,16},{21,... | collective-permute-start | bytes 36872 | tf_op jit(solution)/shard_map/ppermute | solution.py:15
  90.3 2.8 %copy-start.9 = (f32[1,32,8,128]{3,2,1,0:T(8,128)S(1)}, f32[1,32,8,128]{3,2,1,0:T(8,128)}, u32[]{:S(2)}) copy-start(f32[1,32,8,128]{3,2,1,0:T(8,128)} %copy-done.8) | copy-start | bytes 393220
  90.3 2.8 %copy-start.12 = (f32[1,32,8,128]{3,2,1,0:T(8,128)S(1)}, f32[1,32,8,128]{3,2,1,0:T(8,128)}, u32[]{:S(2)}) copy-start(f32[1,32,8,128]{3,2,1,0:T(8,128)} %copy-done.11) | copy-start | bytes 393220
  90.3 2.8 %copy-start.15 = (f32[1,32,8,128]{3,2,1,0:T(8,128)S(1)}, f32[1,32,8,128]{3,2,1,0:T(8,128)}, u32[]{:S(2)}) copy-start(f32[1,32,8,128]{3,2,1,0:T(8,128)} %copy-done.14) | copy-start | bytes 393220
  90.3 2.8 %copy-start.18 = (f32[3,32,8]{2,1,0:T(8,128)S(1)}, f32[3,32,8]{2,1,0:T(8,128)}, u32[]{:S(2)}) copy-start(f32[3,32,8]{2,1,0:T(8,128)} %copy-done.17) | copy-start | bytes 9220
  90.3 2.8 %copy-start.21 = (f32[3,32,8]{2,1,0:T(8,128)S(1)}, f32[3,32,8]{2,1,0:T(8,128)}, u32[]{:S(2)}) copy-start(f32[3,32,8]{2,1,0:T(8,128)} %copy-done.20) | copy-start | bytes 9220
  94.3 0.9 copy-start.7
  95.2 8.0 %copy-start.5 = (f32[3,32,8,128]{3,2,1,0:T(8,128)S(1)}, f32[3,32,8,128]{3,2,1,0:T(8,128)}, u32[]{:S(2)}) copy-start(f32[3,32,8,128]{3,2,1,0:T(8,128)} %copy-done.4) | copy-start | bytes 1179652
  95.4 9.2 %collective-permute-start.22 = (f32[3,32,1,128]{3,2,1,0:T(1,128)S(1)}, f32[3,32,1,128]{3,2,1,0:T(1,128)S(1)}, u32[]{:S(2)}, u32[]{:S(2)}) collective-permute-start(f32[3,32,1,128]{3,2,1,0:T(1,128)S(1)} %slice.768), channel_id=1, source_target_pairs={{0,1},{1,2},{2,3},{4,5},{5,6},{6,7},{8,9},{9,10},{10,11},{12,13},{... | collective-permute-start | bytes 147464 | tf_op jit(solution)/shard_map/ppermute | solution.py:15
  100.0 4.7 %collective-permute-start.23 = (f32[3,1,8,128]{3,2,1,0:T(8,128)S(1)}, f32[3,1,8,128]{3,2,1,0:T(8,128)S(1)}, u32[]{:S(2)}, u32[]{:S(2)}) collective-permute-start(f32[3,1,8,128]{3,2,1,0:T(8,128)S(1)} %slice.774), channel_id=1, source_target_pairs={{0,4},{1,5},{2,6},{3,7},{8,12},{9,13},{10,14},{11,15},{16,20},{17,... | collective-permute-start | bytes 36872 | tf_op jit(solution)/shard_map/ppermute | solution.py:15
  104.9 0.9 copy-start.23
  104.9 0.9 copy-start.25
  105.0 0.8 copy-start.28
  106.5 12.5 %copy-start.19 = (f32[3,32,8]{2,1,0:T(8,128)S(1)}, f32[3,32,8]{2,1,0:T(8,128)}, u32[]{:S(2)}) copy-start(f32[3,32,8]{2,1,0:T(8,128)} %copy-done.17) | copy-start | bytes 9220
  106.5 12.5 %copy-start.22 = (f32[3,32,8]{2,1,0:T(8,128)S(1)}, f32[3,32,8]{2,1,0:T(8,128)}, u32[]{:S(2)}) copy-start(f32[3,32,8]{2,1,0:T(8,128)} %copy-done.20) | copy-start | bytes 9220
  118.1 0.9 copy-start.13
  118.1 1.0 copy-start.16
  118.2 0.9 copy-start.10
  (5 other events, 3.6 us)
where the time goes:
time: 121 us; the launch traced here: 120 us
  starting transfers between devices  58 us (48%)
  waiting for transfers between devices  19.5 us (16%)
  blocking collectives  17.8 us (15%)
  local copies, waits for them, and re-layouts  13.3 us (11%)
  other arithmetic  8.24 us (7%)
  between operations  3.44 us (3%)
    ppermute x24, starting transfers between devices, shifted_2(): return lax.ppermute(block, axis, route)  58 us
    ppermute x24, waiting for transfers between devices, shifted_2(): return lax.ppermute(block, axis, route)  19.5 us
    psum x1, blocking collectives, per_device(): summed = lax.psum(local_grad, 'wl')  11.6 us
    all_gather x1, blocking collectives, per_device(): tiles = lax.all_gather(design, 'wl', axis=0, tiled=True)  6.17 us
    unnamed x59, local copies, waits for them, and re-layouts  5.58 us
    slice x12, local copies, waits for them, and re-layouts, neighbours(): plane_y = stacked[:, :, :1] if upward else stacked[:, :, -1:]  3.04 us
  transfers between devices with their start and end apart: 24, of which 8 were waited for; matrix products, arithmetic and copies ran while one was open for 6% of the time, Pallas kernels for 0%

commit v1 on v0

--- a/solution.py
+++ b/solution.py
@@ -108,7 +108,7 @@
         slab_depth,
     )
     local_grad = jnp.transpose(omega * omega * total, (2, 0, 1))
-    summed = lax.psum(local_grad, "wl")
+    summed = jnp.sum(lax.all_gather(local_grad, "wl"), axis=0)
     gradient = lax.dynamic_slice_in_dim(summed, lax.axis_index("wl") * owned, owned, 0)
     return (efield[None], adj_e[None], gradient)
 

time: 121 us -> 115 us (0.950)
  blocking collectives: 17.8 us -> 11.7 us
    psum x1 -> x0, blocking collectives: 11.6 us -> none  [per_device(): summed = lax.psum(local_grad, 'wl')]
    all_gather x0 -> x1, blocking collectives: none -> 5.55 us  [per_device(): summed = jnp.sum(lax.all_gather(local_grad, 'wl'), axis=0)]
    unnamed x59 -> x58, local copies, waits for them, and re-layouts: 5.58 us -> 4.93 us
where the time goes in v1:
time: 115 us; the launch traced here: 114 us
  starting transfers between devices  58 us (50%)
  waiting for transfers between devices  19.5 us (17%)
  local copies, waits for them, and re-layouts  13.3 us (12%)
  blocking collectives  11.7 us (10%)
  other arithmetic  8.26 us (7%)
  between operations  3.41 us (3%)
    ppermute x24, starting transfers between devices, shifted_2(): return lax.ppermute(block, axis, route)  58 us
    ppermute x24, waiting for transfers between devices, shifted_2(): return lax.ppermute(block, axis, route)  19.5 us
    all_gather x1, blocking collectives, per_device(): tiles = lax.all_gather(design, 'wl', axis=0, tiled=True)  6.17 us
    all_gather x1, blocking collectives, per_device(): summed = jnp.sum(lax.all_gather(local_grad, 'wl'), axis=0)  5.55 us
    unnamed x58, local copies, waits for them, and re-layouts  4.93 us
    slice x12, local copies, waits for them, and re-layouts, neighbours(): plane_y = stacked[:, :, :1] if upward else stacked[:, :, -1:]  3.04 us
  transfers between devices with their start and end apart: 24, of which 8 were waited for; matrix products, arithmetic and copies ran while one was open for 6% of the time, Pallas kernels for 0%

profile of v1, /device:TPU:0, one launch (start us, length us, event | category | flops | bytes accessed | tf_op | source)
XLA Modules:
  0.0 114.2 jit_solution(13119542429207054553)
XLA Ops:
  0.6 1.0 slice.645
  1.7 1.3 %collective-permute-start = (f32[3,32,1,128]{3,2,1,0:T(1,128)S(1)}, f32[3,32,1,128]{3,2,1,0:T(1,128)S(1)}, u32[]{:S(2)}, u32[]{:S(2)}) collective-permute-start(f32[3,32,1,128]{3,2,1,0:T(1,128)S(1)} %slice.645), channel_id=1, source_target_pairs={{1,0},{2,1},{3,2},{5,4},{6,5},{7,6},{9,8},{10,9},{11,10},{13,12},{... | collective-permute-start | bytes 147464 | tf_op jit(solution)/shard_map/ppermute | solution.py:15
  3.0 0.7 slice.651
  3.7 1.3 %collective-permute-start.1 = (f32[3,1,8,128]{3,2,1,0:T(8,128)S(1)}, f32[3,1,8,128]{3,2,1,0:T(8,128)S(1)}, u32[]{:S(2)}, u32[]{:S(2)}) collective-permute-start(f32[3,1,8,128]{3,2,1,0:T(8,128)S(1)} %slice.651), channel_id=1, source_target_pairs={{4,0},{5,1},{6,2},{7,3},{12,8},{13,9},{14,10},{15,11},{20,16},{21,... | collective-permute-start | bytes 36872 | tf_op jit(solution)/shard_map/ppermute | solution.py:15
  5.0 1.0 slice.714
  6.0 1.4 %collective-permute-start.12 = (f32[3,32,1,128]{3,2,1,0:T(1,128)S(1)}, f32[3,32,1,128]{3,2,1,0:T(1,128)S(1)}, u32[]{:S(2)}, u32[]{:S(2)}) collective-permute-start(f32[3,32,1,128]{3,2,1,0:T(1,128)S(1)} %slice.714), channel_id=1, source_target_pairs={{1,0},{2,1},{3,2},{5,4},{6,5},{7,6},{9,8},{10,9},{11,10},{13,12},{... | collective-permute-start | bytes 147464 | tf_op jit(solution)/shard_map/ppermute | solution.py:15
  7.4 0.7 slice.720
  8.2 1.3 %collective-permute-start.13 = (f32[3,1,8,128]{3,2,1,0:T(8,128)S(1)}, f32[3,1,8,128]{3,2,1,0:T(8,128)S(1)}, u32[]{:S(2)}, u32[]{:S(2)}) collective-permute-start(f32[3,1,8,128]{3,2,1,0:T(8,128)S(1)} %slice.720), channel_id=1, source_target_pairs={{4,0},{5,1},{6,2},{7,3},{12,8},{13,9},{14,10},{15,11},{20,16},{21,... | collective-permute-start | bytes 36872 | tf_op jit(solution)/shard_map/ppermute | solution.py:15
  9.5 6.2 %all_gather.9 = f32[8,32,8]{1,2,0:T(8,128)S(1)} all-gather(f32[2,32,8]{1,2,0:T(8,128)S(1)} %copy-done.26), channel_id=1, replica_groups=mesh['wl'=4,'gx'=2,'gy'=4] {'wl'}, dimensions={0}, use_global_device_ids=true | all-gather | bytes 10240 | tf_op jit(solution)/shard_map/all_gather | solution.py:83
  17.6 1.0 copy-done
  20.1 0.9 copy-done.1
  21.1 5.2 %collective-permute-start.2 = (f32[3,32,1,128]{3,2,1,0:T(1,128)S(1)}, f32[3,32,1,128]{3,2,1,0:T(1,128)S(1)}, u32[]{:S(2)}, u32[]{:S(2)}) collective-permute-start(f32[3,32,1,128]{3,2,1,0:T(1,128)S(1)} %slice.655), channel_id=1, source_target_pairs={{0,1},{1,2},{2,3},{4,5},{5,6},{6,7},{8,9},{9,10},{10,11},{12,13},{... | collective-permute-start | bytes 147464 | tf_op jit(solution)/shard_map/ppermute | solution.py:15
  26.3 4.5 %collective-permute-start.3 = (f32[3,1,8,128]{3,2,1,0:T(8,128)S(1)}, f32[3,1,8,128]{3,2,1,0:T(8,128)S(1)}, u32[]{:S(2)}, u32[]{:S(2)}) collective-permute-start(f32[3,1,8,128]{3,2,1,0:T(8,128)S(1)} %slice.661), channel_id=1, source_target_pairs={{0,4},{1,5},{2,6},{3,7},{8,12},{9,13},{10,14},{11,15},{16,20},{17,... | collective-permute-start | bytes 36872 | tf_op jit(solution)/shard_map/ppermute | solution.py:15
  31.1 1.2 %collective-permute-done.3 = f32[3,1,8,128]{3,2,1,0:T(8,128)S(1)} collective-permute-done((f32[3,1,8,128]{3,2,1,0:T(8,128)S(1)}, f32[3,1,8,128]{3,2,1,0:T(8,128)S(1)}, u32[]{:S(2)}, u32[]{:S(2)}) %collective-permute-start.3) | collective-permute-done | bytes 12320 | tf_op jit(solution)/shard_map/ppermute | solution.py:15
  32.7 1.3 %collective-permute-start.4 = (f32[3,32,1,128]{3,2,1,0:T(1,128)S(1)}, f32[3,32,1,128]{3,2,1,0:T(1,128)S(1)}, u32[]{:S(2)}, u32[]{:S(2)}) collective-permute-start(f32[3,32,1,128]{3,2,1,0:T(1,128)S(1)} %slice.668), channel_id=1, source_target_pairs={{1,0},{2,1},{3,2},{5,4},{6,5},{7,6},{9,8},{10,9},{11,10},{13,12},{... | collective-permute-start | bytes 147464 | tf_op jit(solution)/shard_map/ppermute | solution.py:15
  34.0 1.3 %collective-permute-start.5 = (f32[3,1,8,128]{3,2,1,0:T(8,128)S(1)}, f32[3,1,8,128]{3,2,1,0:T(8,128)S(1)}, u32[]{:S(2)}, u32[]{:S(2)}) collective-permute-start(f32[3,1,8,128]{3,2,1,0:T(8,128)S(1)} %slice.674), channel_id=1, source_target_pairs={{4,0},{5,1},{6,2},{7,3},{12,8},{13,9},{14,10},{15,11},{20,16},{21,... | collective-permute-start | bytes 36872 | tf_op jit(solution)/shard_map/ppermute | solution.py:15
  35.6 4.0 %collective-permute-done.5 = f32[3,1,8,128]{3,2,1,0:T(8,128)S(1)} collective-permute-done((f32[3,1,8,128]{3,2,1,0:T(8,128)S(1)}, f32[3,1,8,128]{3,2,1,0:T(8,128)S(1)}, u32[]{:S(2)}, u32[]{:S(2)}) %collective-permute-start.5) | collective-permute-done | bytes 12320 | tf_op jit(solution)/shard_map/ppermute | solution.py:15
  40.0 4.6 %collective-permute-start.6 = (f32[3,32,1,128]{3,2,1,0:T(1,128)S(1)}, f32[3,32,1,128]{3,2,1,0:T(1,128)S(1)}, u32[]{:S(2)}, u32[]{:S(2)}) collective-permute-start(f32[3,32,1,128]{3,2,1,0:T(1,128)S(1)} %slice.678), channel_id=1, source_target_pairs={{0,1},{1,2},{2,3},{4,5},{5,6},{6,7},{8,9},{9,10},{10,11},{12,13},{... | collective-permute-start | bytes 147464 | tf_op jit(solution)/shard_map/ppermute | solution.py:15
  44.5 2.7 %collective-permute-start.7 = (f32[3,1,8,128]{3,2,1,0:T(8,128)S(1)}, f32[3,1,8,128]{3,2,1,0:T(8,128)S(1)}, u32[]{:S(2)}, u32[]{:S(2)}) collective-permute-start(f32[3,1,8,128]{3,2,1,0:T(8,128)S(1)} %slice.684), channel_id=1, source_target_pairs={{0,4},{1,5},{2,6},{3,7},{8,12},{9,13},{10,14},{11,15},{16,20},{17,... | collective-permute-start | bytes 36872 | tf_op jit(solution)/shard_map/ppermute | solution.py:15
  47.4 3.9 %collective-permute-start.14 = (f32[3,32,1,128]{3,2,1,0:T(1,128)S(1)}, f32[3,32,1,128]{3,2,1,0:T(1,128)S(1)}, u32[]{:S(2)}, u32[]{:S(2)}) collective-permute-start(f32[3,32,1,128]{3,2,1,0:T(1,128)S(1)} %slice.724), channel_id=1, source_target_pairs={{0,1},{1,2},{2,3},{4,5},{5,6},{6,7},{8,9},{9,10},{10,11},{12,13},{... | collective-permute-start | bytes 147464 | tf_op jit(solution)/shard_map/ppermute | solution.py:15
  51.3 1.3 %collective-permute-start.15 = (f32[3,1,8,128]{3,2,1,0:T(8,128)S(1)}, f32[3,1,8,128]{3,2,1,0:T(8,128)S(1)}, u32[]{:S(2)}, u32[]{:S(2)}) collective-permute-start(f32[3,1,8,128]{3,2,1,0:T(8,128)S(1)} %slice.730), channel_id=1, source_target_pairs={{0,4},{1,5},{2,6},{3,7},{8,12},{9,13},{10,14},{11,15},{16,20},{17,... | collective-permute-start | bytes 36872 | tf_op jit(solution)/shard_map/ppermute | solution.py:15
  53.1 1.3 %collective-permute-start.8 = (f32[3,32,1,128]{3,2,1,0:T(1,128)S(1)}, f32[3,32,1,128]{3,2,1,0:T(1,128)S(1)}, u32[]{:S(2)}, u32[]{:S(2)}) collective-permute-start(f32[3,32,1,128]{3,2,1,0:T(1,128)S(1)} %slice.691), channel_id=1, source_target_pairs={{1,0},{2,1},{3,2},{5,4},{6,5},{7,6},{9,8},{10,9},{11,10},{13,12},{... | collective-permute-start | bytes 147464 | tf_op jit(solution)/shard_map/ppermute | solution.py:15
  54.4 1.3 %collective-permute-start.9 = (f32[3,1,8,128]{3,2,1,0:T(8,128)S(1)}, f32[3,1,8,128]{3,2,1,0:T(8,128)S(1)}, u32[]{:S(2)}, u32[]{:S(2)}) collective-permute-start(f32[3,1,8,128]{3,2,1,0:T(8,128)S(1)} %slice.697), channel_id=1, source_target_pairs={{4,0},{5,1},{6,2},{7,3},{12,8},{13,9},{14,10},{15,11},{20,16},{21,... | collective-permute-start | bytes 36872 | tf_op jit(solution)/shard_map/ppermute | solution.py:15
  56.2 3.8 %collective-permute-done.9 = f32[3,1,8,128]{3,2,1,0:T(8,128)S(1)} collective-permute-done((f32[3,1,8,128]{3,2,1,0:T(8,128)S(1)}, f32[3,1,8,128]{3,2,1,0:T(8,128)S(1)}, u32[]{:S(2)}, u32[]{:S(2)}) %collective-permute-start.9) | collective-permute-done | bytes 12320 | tf_op jit(solution)/shard_map/ppermute | solution.py:15
  60.4 4.5 %collective-permute-start.10 = (f32[3,32,1,128]{3,2,1,0:T(1,128)S(1)}, f32[3,32,1,128]{3,2,1,0:T(1,128)S(1)}, u32[]{:S(2)}, u32[]{:S(2)}) collective-permute-start(f32[3,32,1,128]{3,2,1,0:T(1,128)S(1)} %slice.701), channel_id=1, source_target_pairs={{0,1},{1,2},{2,3},{4,5},{5,6},{6,7},{8,9},{9,10},{10,11},{12,13},{... | collective-permute-start | bytes 147464 | tf_op jit(solution)/shard_map/ppermute | solution.py:15
  64.9 1.6 %collective-permute-start.11 = (f32[3,1,8,128]{3,2,1,0:T(8,128)S(1)}, f32[3,1,8,128]{3,2,1,0:T(8,128)S(1)}, u32[]{:S(2)}, u32[]{:S(2)}) collective-permute-start(f32[3,1,8,128]{3,2,1,0:T(8,128)S(1)} %slice.707), channel_id=1, source_target_pairs={{0,4},{1,5},{2,6},{3,7},{8,12},{9,13},{10,14},{11,15},{16,20},{17,... | collective-permute-start | bytes 36872 | tf_op jit(solution)/shard_map/ppermute | solution.py:15
  66.7 1.3 %collective-permute-done.11 = f32[3,1,8,128]{3,2,1,0:T(8,128)S(1)} collective-permute-done((f32[3,1,8,128]{3,2,1,0:T(8,128)S(1)}, f32[3,1,8,128]{3,2,1,0:T(8,128)S(1)}, u32[]{:S(2)}, u32[]{:S(2)}) %collective-permute-start.11) | collective-permute-done | bytes 12320 | tf_op jit(solution)/shard_map/ppermute | solution.py:15
  68.5 0.8 multiply_reduce_fusion
  69.5 1.3 %collective-permute-start.16 = (f32[3,32,1,128]{3,2,1,0:T(1,128)S(1)}, f32[3,32,1,128]{3,2,1,0:T(1,128)S(1)}, u32[]{:S(2)}, u32[]{:S(2)}) collective-permute-start(f32[3,32,1,128]{3,2,1,0:T(1,128)S(1)} %slice.736), channel_id=1, source_target_pairs={{1,0},{2,1},{3,2},{5,4},{6,5},{7,6},{9,8},{10,9},{11,10},{13,12},{... | collective-permute-start | bytes 147464 | tf_op jit(solution)/shard_map/ppermute | solution.py:15
  70.8 1.3 %collective-permute-start.17 = (f32[3,1,8,128]{3,2,1,0:T(8,128)S(1)}, f32[3,1,8,128]{3,2,1,0:T(8,128)S(1)}, u32[]{:S(2)}, u32[]{:S(2)}) collective-permute-start(f32[3,1,8,128]{3,2,1,0:T(8,128)S(1)} %slice.742), channel_id=1, source_target_pairs={{4,0},{5,1},{6,2},{7,3},{12,8},{13,9},{14,10},{15,11},{20,16},{21,... | collective-permute-start | bytes 36872 | tf_op jit(solution)/shard_map/ppermute | solution.py:15
  72.4 4.0 %collective-permute-done.17 = f32[3,1,8,128]{3,2,1,0:T(8,128)S(1)} collective-permute-done((f32[3,1,8,128]{3,2,1,0:T(8,128)S(1)}, f32[3,1,8,128]{3,2,1,0:T(8,128)S(1)}, u32[]{:S(2)}, u32[]{:S(2)}) %collective-permute-start.17) | collective-permute-done | bytes 12320 | tf_op jit(solution)/shard_map/ppermute | solution.py:15
  76.9 4.5 %collective-permute-start.18 = (f32[3,32,1,128]{3,2,1,0:T(1,128)S(1)}, f32[3,32,1,128]{3,2,1,0:T(1,128)S(1)}, u32[]{:S(2)}, u32[]{:S(2)}) collective-permute-start(f32[3,32,1,128]{3,2,1,0:T(1,128)S(1)} %slice.746), channel_id=1, source_target_pairs={{0,1},{1,2},{2,3},{4,5},{5,6},{6,7},{8,9},{9,10},{10,11},{12,13},{... | collective-permute-start | bytes 147464 | tf_op jit(solution)/shard_map/ppermute | solution.py:15
  81.4 1.6 %collective-permute-start.19 = (f32[3,1,8,128]{3,2,1,0:T(8,128)S(1)}, f32[3,1,8,128]{3,2,1,0:T(8,128)S(1)}, u32[]{:S(2)}, u32[]{:S(2)}) collective-permute-start(f32[3,1,8,128]{3,2,1,0:T(8,128)S(1)} %slice.752), channel_id=1, source_target_pairs={{0,4},{1,5},{2,6},{3,7},{8,12},{9,13},{10,14},{11,15},{16,20},{17,... | collective-permute-start | bytes 36872 | tf_op jit(solution)/shard_map/ppermute | solution.py:15
  83.1 1.4 %collective-permute-done.19 = f32[3,1,8,128]{3,2,1,0:T(8,128)S(1)} collective-permute-done((f32[3,1,8,128]{3,2,1,0:T(8,128)S(1)}, f32[3,1,8,128]{3,2,1,0:T(8,128)S(1)}, u32[]{:S(2)}, u32[]{:S(2)}) %collective-permute-start.19) | collective-permute-done | bytes 12320 | tf_op jit(solution)/shard_map/ppermute | solution.py:15
  85.5 0.6 slice.758
  86.1 1.3 %collective-permute-start.20 = (f32[3,32,1,128]{3,2,1,0:T(1,128)}, f32[3,32,1,128]{3,2,1,0:T(1,128)}, u32[]{:S(2)}, u32[]{:S(2)}) collective-permute-start(f32[3,32,1,128]{3,2,1,0:T(1,128)} %slice.758), channel_id=1, source_target_pairs={{1,0},{2,1},{3,2},{5,4},{6,5},{7,6},{9,8},{10,9},{11,10},{13,12},{... | collective-permute-start | bytes 147464 | tf_op jit(solution)/shard_map/ppermute | solution.py:15
  87.4 1.3 %collective-permute-start.21 = (f32[3,1,8,128]{3,2,1,0:T(8,128)S(1)}, f32[3,1,8,128]{3,2,1,0:T(8,128)}, u32[]{:S(2)}, u32[]{:S(2)}) collective-permute-start(f32[3,1,8,128]{3,2,1,0:T(8,128)S(1)} %slice.764), channel_id=1, source_target_pairs={{4,0},{5,1},{6,2},{7,3},{12,8},{13,9},{14,10},{15,11},{20,16},{21,... | collective-permute-start | bytes 36872 | tf_op jit(solution)/shard_map/ppermute | solution.py:15
  88.7 0.8 slice.784
  90.4 2.8 %collective-permute-done.21 = f32[3,1,8,128]{3,2,1,0:T(8,128)} collective-permute-done((f32[3,1,8,128]{3,2,1,0:T(8,128)S(1)}, f32[3,1,8,128]{3,2,1,0:T(8,128)}, u32[]{:S(2)}, u32[]{:S(2)}) %collective-permute-start.21) | collective-permute-done | bytes 12320 | tf_op jit(solution)/shard_map/ppermute | solution.py:15
  93.2 1.2 %pad_subtract_fusion.1 = (f32[3,32,8,128]{3,2,1,0:T(8,128)S(1)}, f32[3,32,8,128]{3,2,1,0:T(8,128)S(1)}, f32[3,32,8,128]{3,2,1,0:T(8,128)S(1)}) fusion(f32[3,32,8,127]{3,2,1,0:T(8,128)S(1)} %slice.760, f32[3,1,8,128]{3,2,1,0:T(8,128)} %collective-permute-done.21, f32[3,31,8,128]{3,2,1,0:T(8,128)S(1)} %slice.763, ...), kind=kLoop, calls=%fused_computation.70 | loop fusion | flops 1671168 | bytes 3673600 | tf_op jit(solution)/shard_map/sub | solution.py:31
  94.4 0.8 copy-done.7
  95.4 4.5 %collective-permute-start.22 = (f32[3,32,1,128]{3,2,1,0:T(1,128)S(1)}, f32[3,32,1,128]{3,2,1,0:T(1,128)S(1)}, u32[]{:S(2)}, u32[]{:S(2)}) collective-permute-start(f32[3,32,1,128]{3,2,1,0:T(1,128)S(1)} %slice.768), channel_id=1, source_target_pairs={{0,1},{1,2},{2,3},{4,5},{5,6},{6,7},{8,9},{9,10},{10,11},{12,13},{... | collective-permute-start | bytes 147464 | tf_op jit(solution)/shard_map/ppermute | solution.py:15
  100.0 3.3 %collective-permute-start.23 = (f32[3,1,8,128]{3,2,1,0:T(8,128)S(1)}, f32[3,1,8,128]{3,2,1,0:T(8,128)S(1)}, u32[]{:S(2)}, u32[]{:S(2)}) collective-permute-start(f32[3,1,8,128]{3,2,1,0:T(8,128)S(1)} %slice.774), channel_id=1, source_target_pairs={{0,4},{1,5},{2,6},{3,7},{8,12},{9,13},{10,14},{11,15},{16,20},{17,... | collective-permute-start | bytes 36872 | tf_op jit(solution)/shard_map/ppermute | solution.py:15
  103.6 1.1 collective-permute-done.23
  105.0 0.8 copy-done.23
  106.6 5.6 %all-gather = f32[32,32,8]{1,2,0:T(8,128)S(1)} all-gather(f32[8,32,8]{1,2,0:T(8,128)S(1)} %copy.18), channel_id=2, replica_groups=mesh['wl'=4,'gx'=2,'gy'=4] {'wl'}, dimensions={0}, use_global_device_ids=true | all-gather | bytes 40960 | tf_op jit(solution)/shard_map/all_gather | solution.py:111
  112.2 0.6 constant_dynamic-slice_fusion
  113.1 1.1 fusion.19
  (162 shorter events, 9.5 us)
Async XLA Ops:
  1.7 18.2 %collective-permute-start = (f32[3,32,1,128]{3,2,1,0:T(1,128)S(1)}, f32[3,32,1,128]{3,2,1,0:T(1,128)S(1)}, u32[]{:S(2)}, u32[]{:S(2)}) collective-permute-start(f32[3,32,1,128]{3,2,1,0:T(1,128)S(1)} %slice.645), channel_id=1, source_target_pairs={{1,0},{2,1},{3,2},{5,4},{6,5},{7,6},{9,8},{10,9},{11,10},{13,12},{... | collective-permute-start | bytes 147464 | tf_op jit(solution)/shard_map/ppermute | solution.py:15
  3.7 16.2 %collective-permute-start.1 = (f32[3,1,8,128]{3,2,1,0:T(8,128)S(1)}, f32[3,1,8,128]{3,2,1,0:T(8,128)S(1)}, u32[]{:S(2)}, u32[]{:S(2)}) collective-permute-start(f32[3,1,8,128]{3,2,1,0:T(8,128)S(1)} %slice.651), channel_id=1, source_target_pairs={{4,0},{5,1},{6,2},{7,3},{12,8},{13,9},{14,10},{15,11},{20,16},{21,... | collective-permute-start | bytes 36872 | tf_op jit(solution)/shard_map/ppermute | solution.py:15
  5.0 4.5 %copy-start.26 = (f32[2,32,8]{1,2,0:T(8,128)S(1)}, f32[2,32,8]{1,2,0:T(8,128)}, u32[]{:S(2)}) copy-start(f32[2,32,8]{1,2,0:T(8,128)} %param.20) | copy-start | bytes 6148
  6.0 9.8 %copy-start.24 = (f32[32,8,128]{2,1,0:T(8,128)S(1)}, f32[32,8,128]{2,1,0:T(8,128)}, u32[]{:S(2)}) copy-start(f32[32,8,128]{2,1,0:T(8,128)} %param.19) | copy-start | bytes 393220
  6.0 24.9 %collective-permute-start.12 = (f32[3,32,1,128]{3,2,1,0:T(1,128)S(1)}, f32[3,32,1,128]{3,2,1,0:T(1,128)S(1)}, u32[]{:S(2)}, u32[]{:S(2)}) collective-permute-start(f32[3,32,1,128]{3,2,1,0:T(1,128)S(1)} %slice.714), channel_id=1, source_target_pairs={{1,0},{2,1},{3,2},{5,4},{6,5},{7,6},{9,8},{10,9},{11,10},{13,12},{... | collective-permute-start | bytes 147464 | tf_op jit(solution)/shard_map/ppermute | solution.py:15
  8.2 22.7 %collective-permute-start.13 = (f32[3,1,8,128]{3,2,1,0:T(8,128)S(1)}, f32[3,1,8,128]{3,2,1,0:T(8,128)S(1)}, u32[]{:S(2)}, u32[]{:S(2)}) collective-permute-start(f32[3,1,8,128]{3,2,1,0:T(8,128)S(1)} %slice.720), channel_id=1, source_target_pairs={{4,0},{5,1},{6,2},{7,3},{12,8},{13,9},{14,10},{15,11},{20,16},{21,... | collective-permute-start | bytes 36872 | tf_op jit(solution)/shard_map/ppermute | solution.py:15
  15.8 1.6 %copy-start.3 = (f32[1,3,32,8,128]{4,3,2,1,0:T(8,128)S(1)}, f32[1,3,32,8,128]{4,3,2,1,0:T(8,128)}, u32[]{:S(2)}) copy-start(f32[1,3,32,8,128]{4,3,2,1,0:T(8,128)} %param.15) | copy-start | bytes 1179652
  17.6 1.0 copy-start
  20.0 1.0 copy-start.1
  21.1 11.2 %collective-permute-start.2 = (f32[3,32,1,128]{3,2,1,0:T(1,128)S(1)}, f32[3,32,1,128]{3,2,1,0:T(1,128)S(1)}, u32[]{:S(2)}, u32[]{:S(2)}) collective-permute-start(f32[3,32,1,128]{3,2,1,0:T(1,128)S(1)} %slice.655), channel_id=1, source_target_pairs={{0,1},{1,2},{2,3},{4,5},{5,6},{6,7},{8,9},{9,10},{10,11},{12,13},{... | collective-permute-start | bytes 147464 | tf_op jit(solution)/shard_map/ppermute | solution.py:15
  26.3 5.9 %collective-permute-start.3 = (f32[3,1,8,128]{3,2,1,0:T(8,128)S(1)}, f32[3,1,8,128]{3,2,1,0:T(8,128)S(1)}, u32[]{:S(2)}, u32[]{:S(2)}) collective-permute-start(f32[3,1,8,128]{3,2,1,0:T(8,128)S(1)} %slice.661), channel_id=1, source_target_pairs={{0,4},{1,5},{2,6},{3,7},{8,12},{9,13},{10,14},{11,15},{16,20},{17,... | collective-permute-start | bytes 36872 | tf_op jit(solution)/shard_map/ppermute | solution.py:15
  32.7 6.9 %collective-permute-start.4 = (f32[3,32,1,128]{3,2,1,0:T(1,128)S(1)}, f32[3,32,1,128]{3,2,1,0:T(1,128)S(1)}, u32[]{:S(2)}, u32[]{:S(2)}) collective-permute-start(f32[3,32,1,128]{3,2,1,0:T(1,128)S(1)} %slice.668), channel_id=1, source_target_pairs={{1,0},{2,1},{3,2},{5,4},{6,5},{7,6},{9,8},{10,9},{11,10},{13,12},{... | collective-permute-start | bytes 147464 | tf_op jit(solution)/shard_map/ppermute | solution.py:15
  34.0 5.6 %collective-permute-start.5 = (f32[3,1,8,128]{3,2,1,0:T(8,128)S(1)}, f32[3,1,8,128]{3,2,1,0:T(8,128)S(1)}, u32[]{:S(2)}, u32[]{:S(2)}) collective-permute-start(f32[3,1,8,128]{3,2,1,0:T(8,128)S(1)} %slice.674), channel_id=1, source_target_pairs={{4,0},{5,1},{6,2},{7,3},{12,8},{13,9},{14,10},{15,11},{20,16},{21,... | collective-permute-start | bytes 36872 | tf_op jit(solution)/shard_map/ppermute | solution.py:15
  39.8 7.4 %copy-start.2 = (f32[1,3,32,8,128]{4,3,2,1,0:T(8,128)S(1)}, f32[1,3,32,8,128]{4,3,2,1,0:T(8,128)}, u32[]{:S(2)}) copy-start(f32[1,3,32,8,128]{4,3,2,1,0:T(8,128)} %param.18) | copy-start | bytes 1179652
  40.0 12.7 %collective-permute-start.6 = (f32[3,32,1,128]{3,2,1,0:T(1,128)S(1)}, f32[3,32,1,128]{3,2,1,0:T(1,128)S(1)}, u32[]{:S(2)}, u32[]{:S(2)}) collective-permute-start(f32[3,32,1,128]{3,2,1,0:T(1,128)S(1)} %slice.678), channel_id=1, source_target_pairs={{0,1},{1,2},{2,3},{4,5},{5,6},{6,7},{8,9},{9,10},{10,11},{12,13},{... | collective-permute-start | bytes 147464 | tf_op jit(solution)/shard_map/ppermute | solution.py:15
  44.5 8.1 %collective-permute-start.7 = (f32[3,1,8,128]{3,2,1,0:T(8,128)S(1)}, f32[3,1,8,128]{3,2,1,0:T(8,128)S(1)}, u32[]{:S(2)}, u32[]{:S(2)}) collective-permute-start(f32[3,1,8,128]{3,2,1,0:T(8,128)S(1)} %slice.684), channel_id=1, source_target_pairs={{0,4},{1,5},{2,6},{3,7},{8,12},{9,13},{10,14},{11,15},{16,20},{17,... | collective-permute-start | bytes 36872 | tf_op jit(solution)/shard_map/ppermute | solution.py:15
  47.4 8.4 %collective-permute-start.14 = (f32[3,32,1,128]{3,2,1,0:T(1,128)S(1)}, f32[3,32,1,128]{3,2,1,0:T(1,128)S(1)}, u32[]{:S(2)}, u32[]{:S(2)}) collective-permute-start(f32[3,32,1,128]{3,2,1,0:T(1,128)S(1)} %slice.724), channel_id=1, source_target_pairs={{0,1},{1,2},{2,3},{4,5},{5,6},{6,7},{8,9},{9,10},{10,11},{12,13},{... | collective-permute-start | bytes 147464 | tf_op jit(solution)/shard_map/ppermute | solution.py:15
  51.3 4.5 %collective-permute-start.15 = (f32[3,1,8,128]{3,2,1,0:T(8,128)S(1)}, f32[3,1,8,128]{3,2,1,0:T(8,128)S(1)}, u32[]{:S(2)}, u32[]{:S(2)}) collective-permute-start(f32[3,1,8,128]{3,2,1,0:T(8,128)S(1)} %slice.730), channel_id=1, source_target_pairs={{0,4},{1,5},{2,6},{3,7},{8,12},{9,13},{10,14},{11,15},{16,20},{17,... | collective-permute-start | bytes 36872 | tf_op jit(solution)/shard_map/ppermute | solution.py:15
  53.1 6.9 %collective-permute-start.8 = (f32[3,32,1,128]{3,2,1,0:T(1,128)S(1)}, f32[3,32,1,128]{3,2,1,0:T(1,128)S(1)}, u32[]{:S(2)}, u32[]{:S(2)}) collective-permute-start(f32[3,32,1,128]{3,2,1,0:T(1,128)S(1)} %slice.691), channel_id=1, source_target_pairs={{1,0},{2,1},{3,2},{5,4},{6,5},{7,6},{9,8},{10,9},{11,10},{13,12},{... | collective-permute-start | bytes 147464 | tf_op jit(solution)/shard_map/ppermute | solution.py:15
  54.4 5.6 %collective-permute-start.9 = (f32[3,1,8,128]{3,2,1,0:T(8,128)S(1)}, f32[3,1,8,128]{3,2,1,0:T(8,128)S(1)}, u32[]{:S(2)}, u32[]{:S(2)}) collective-permute-start(f32[3,1,8,128]{3,2,1,0:T(8,128)S(1)} %slice.697), channel_id=1, source_target_pairs={{4,0},{5,1},{6,2},{7,3},{12,8},{13,9},{14,10},{15,11},{20,16},{21,... | collective-permute-start | bytes 36872 | tf_op jit(solution)/shard_map/ppermute | solution.py:15
  60.4 7.6 %collective-permute-start.10 = (f32[3,32,1,128]{3,2,1,0:T(1,128)S(1)}, f32[3,32,1,128]{3,2,1,0:T(1,128)S(1)}, u32[]{:S(2)}, u32[]{:S(2)}) collective-permute-start(f32[3,32,1,128]{3,2,1,0:T(1,128)S(1)} %slice.701), channel_id=1, source_target_pairs={{0,1},{1,2},{2,3},{4,5},{5,6},{6,7},{8,9},{9,10},{10,11},{12,13},{... | collective-permute-start | bytes 147464 | tf_op jit(solution)/shard_map/ppermute | solution.py:15
  64.9 3.0 %collective-permute-start.11 = (f32[3,1,8,128]{3,2,1,0:T(8,128)S(1)}, f32[3,1,8,128]{3,2,1,0:T(8,128)S(1)}, u32[]{:S(2)}, u32[]{:S(2)}) collective-permute-start(f32[3,1,8,128]{3,2,1,0:T(8,128)S(1)} %slice.707), channel_id=1, source_target_pairs={{0,4},{1,5},{2,6},{3,7},{8,12},{9,13},{10,14},{11,15},{16,20},{17,... | collective-permute-start | bytes 36872 | tf_op jit(solution)/shard_map/ppermute | solution.py:15
  69.3 15.5 %copy-start.17 = (f32[3,32,8]{2,1,0:T(8,128)}, f32[3,32,8]{2,1,0:T(8,128)S(1)}, u32[]{:S(2)}) copy-start(f32[3,32,8]{2,1,0:T(8,128)S(1)} %get-tuple-element.43) | copy-start | bytes 9220
  69.3 15.5 %copy-start.20 = (f32[3,32,8]{2,1,0:T(8,128)}, f32[3,32,8]{2,1,0:T(8,128)S(1)}, u32[]{:S(2)}) copy-start(f32[3,32,8]{2,1,0:T(8,128)S(1)} %get-tuple-element.42) | copy-start | bytes 9220
  69.5 6.9 %collective-permute-start.16 = (f32[3,32,1,128]{3,2,1,0:T(1,128)S(1)}, f32[3,32,1,128]{3,2,1,0:T(1,128)S(1)}, u32[]{:S(2)}, u32[]{:S(2)}) collective-permute-start(f32[3,32,1,128]{3,2,1,0:T(1,128)S(1)} %slice.736), channel_id=1, source_target_pairs={{1,0},{2,1},{3,2},{5,4},{6,5},{7,6},{9,8},{10,9},{11,10},{13,12},{... | collective-permute-start | bytes 147464 | tf_op jit(solution)/shard_map/ppermute | solution.py:15
  70.8 5.6 %collective-permute-start.17 = (f32[3,1,8,128]{3,2,1,0:T(8,128)S(1)}, f32[3,1,8,128]{3,2,1,0:T(8,128)S(1)}, u32[]{:S(2)}, u32[]{:S(2)}) collective-permute-start(f32[3,1,8,128]{3,2,1,0:T(8,128)S(1)} %slice.742), channel_id=1, source_target_pairs={{4,0},{5,1},{6,2},{7,3},{12,8},{13,9},{14,10},{15,11},{20,16},{21,... | collective-permute-start | bytes 36872 | tf_op jit(solution)/shard_map/ppermute | solution.py:15
  76.7 7.7 %copy-start.6 = (f32[1,32,8,128]{3,2,1,0:T(8,128)}, f32[1,32,8,128]{3,2,1,0:T(8,128)S(1)}, u32[]{:S(2)}) copy-start(f32[1,32,8,128]{3,2,1,0:T(8,128)S(1)} %get-tuple-element.64) | copy-start | bytes 393220
  76.9 7.6 %collective-permute-start.18 = (f32[3,32,1,128]{3,2,1,0:T(1,128)S(1)}, f32[3,32,1,128]{3,2,1,0:T(1,128)S(1)}, u32[]{:S(2)}, u32[]{:S(2)}) collective-permute-start(f32[3,32,1,128]{3,2,1,0:T(1,128)S(1)} %slice.746), channel_id=1, source_target_pairs={{0,1},{1,2},{2,3},{4,5},{5,6},{6,7},{8,9},{9,10},{10,11},{12,13},{... | collective-permute-start | bytes 147464 | tf_op jit(solution)/shard_map/ppermute | solution.py:15
  81.4 3.0 %collective-permute-start.19 = (f32[3,1,8,128]{3,2,1,0:T(8,128)S(1)}, f32[3,1,8,128]{3,2,1,0:T(8,128)S(1)}, u32[]{:S(2)}, u32[]{:S(2)}) collective-permute-start(f32[3,1,8,128]{3,2,1,0:T(8,128)S(1)} %slice.752), channel_id=1, source_target_pairs={{0,4},{1,5},{2,6},{3,7},{8,12},{9,13},{10,14},{11,15},{16,20},{17,... | collective-permute-start | bytes 36872 | tf_op jit(solution)/shard_map/ppermute | solution.py:15
  86.1 7.0 %collective-permute-start.20 = (f32[3,32,1,128]{3,2,1,0:T(1,128)}, f32[3,32,1,128]{3,2,1,0:T(1,128)}, u32[]{:S(2)}, u32[]{:S(2)}) collective-permute-start(f32[3,32,1,128]{3,2,1,0:T(1,128)} %slice.758), channel_id=1, source_target_pairs={{1,0},{2,1},{3,2},{5,4},{6,5},{7,6},{9,8},{10,9},{11,10},{13,12},{... | collective-permute-start | bytes 147464 | tf_op jit(solution)/shard_map/ppermute | solution.py:15
  87.4 5.7 %collective-permute-start.21 = (f32[3,1,8,128]{3,2,1,0:T(8,128)S(1)}, f32[3,1,8,128]{3,2,1,0:T(8,128)}, u32[]{:S(2)}, u32[]{:S(2)}) collective-permute-start(f32[3,1,8,128]{3,2,1,0:T(8,128)S(1)} %slice.764), channel_id=1, source_target_pairs={{4,0},{5,1},{6,2},{7,3},{12,8},{13,9},{14,10},{15,11},{20,16},{21,... | collective-permute-start | bytes 36872 | tf_op jit(solution)/shard_map/ppermute | solution.py:15
  90.3 2.8 %copy-start.9 = (f32[1,32,8,128]{3,2,1,0:T(8,128)S(1)}, f32[1,32,8,128]{3,2,1,0:T(8,128)}, u32[]{:S(2)}) copy-start(f32[1,32,8,128]{3,2,1,0:T(8,128)} %copy-done.8) | copy-start | bytes 393220
  90.3 2.8 %copy-start.12 = (f32[1,32,8,128]{3,2,1,0:T(8,128)S(1)}, f32[1,32,8,128]{3,2,1,0:T(8,128)}, u32[]{:S(2)}) copy-start(f32[1,32,8,128]{3,2,1,0:T(8,128)} %copy-done.11) | copy-start | bytes 393220
  90.3 2.8 %copy-start.15 = (f32[1,32,8,128]{3,2,1,0:T(8,128)S(1)}, f32[1,32,8,128]{3,2,1,0:T(8,128)}, u32[]{:S(2)}) copy-start(f32[1,32,8,128]{3,2,1,0:T(8,128)} %copy-done.14) | copy-start | bytes 393220
  90.3 2.8 %copy-start.18 = (f32[3,32,8]{2,1,0:T(8,128)S(1)}, f32[3,32,8]{2,1,0:T(8,128)}, u32[]{:S(2)}) copy-start(f32[3,32,8]{2,1,0:T(8,128)} %copy-done.17) | copy-start | bytes 9220
  90.3 2.8 %copy-start.21 = (f32[3,32,8]{2,1,0:T(8,128)S(1)}, f32[3,32,8]{2,1,0:T(8,128)}, u32[]{:S(2)}) copy-start(f32[3,32,8]{2,1,0:T(8,128)} %copy-done.20) | copy-start | bytes 9220
  94.3 0.9 copy-start.7
  95.2 8.0 %copy-start.5 = (f32[3,32,8,128]{3,2,1,0:T(8,128)S(1)}, f32[3,32,8,128]{3,2,1,0:T(8,128)}, u32[]{:S(2)}) copy-start(f32[3,32,8,128]{3,2,1,0:T(8,128)} %copy-done.4) | copy-start | bytes 1179652
  95.4 9.2 %collective-permute-start.22 = (f32[3,32,1,128]{3,2,1,0:T(1,128)S(1)}, f32[3,32,1,128]{3,2,1,0:T(1,128)S(1)}, u32[]{:S(2)}, u32[]{:S(2)}) collective-permute-start(f32[3,32,1,128]{3,2,1,0:T(1,128)S(1)} %slice.768), channel_id=1, source_target_pairs={{0,1},{1,2},{2,3},{4,5},{5,6},{6,7},{8,9},{9,10},{10,11},{12,13},{... | collective-permute-start | bytes 147464 | tf_op jit(solution)/shard_map/ppermute | solution.py:15
  100.0 4.7 %collective-permute-start.23 = (f32[3,1,8,128]{3,2,1,0:T(8,128)S(1)}, f32[3,1,8,128]{3,2,1,0:T(8,128)S(1)}, u32[]{:S(2)}, u32[]{:S(2)}) collective-permute-start(f32[3,1,8,128]{3,2,1,0:T(8,128)S(1)} %slice.774), channel_id=1, source_target_pairs={{0,4},{1,5},{2,6},{3,7},{8,12},{9,13},{10,14},{11,15},{16,20},{17,... | collective-permute-start | bytes 36872 | tf_op jit(solution)/shard_map/ppermute | solution.py:15
  104.9 0.9 copy-start.23
  104.9 0.9 copy-start.25
  105.0 0.8 copy-start.28
  106.4 6.3 %copy-start.16 = (f32[1,32,8,128]{3,2,1,0:T(8,128)S(1)}, f32[1,32,8,128]{3,2,1,0:T(8,128)}, u32[]{:S(2)}) copy-start(f32[1,32,8,128]{3,2,1,0:T(8,128)} %copy-done.14) | copy-start | bytes 393220
  106.5 6.3 %copy-start.22 = (f32[3,32,8]{2,1,0:T(8,128)S(1)}, f32[3,32,8]{2,1,0:T(8,128)}, u32[]{:S(2)}) copy-start(f32[3,32,8]{2,1,0:T(8,128)} %copy-done.20) | copy-start | bytes 9220
  106.6 6.2 %copy-start.13 = (f32[1,32,8,128]{3,2,1,0:T(8,128)S(1)}, f32[1,32,8,128]{3,2,1,0:T(8,128)}, u32[]{:S(2)}) copy-start(f32[1,32,8,128]{3,2,1,0:T(8,128)} %copy-done.11) | copy-start | bytes 393220
  112.1 0.9 copy-start.10
  112.1 0.9 copy-start.19
  (5 other events, 3.6 us)
